TPU v7x, 32 devices: a whole 2x2x4 slice. The times are simulated.
32 devices in a mesh: groups: 2 (over y), depth: 4 (over z), rows: 2 (over x), cols: 2 (over core).
Axes of the slice: x: 2, y: 2, z: 4, core: 2. Of those that a mesh axis runs over, the one named last changes fastest.
Arguments:
- volume: bfloat16 [4, 16, 16, 3072], P('groups', 'depth', 'rows', 'cols'), parts along dimension 0, may hold values from -6 to 6
- grad_out: bfloat16 [4, 16, 16, 3072], P('groups', 'depth', 'rows', 'cols'), parts along dimension 0, may hold values from -6 to 6
- report: bfloat16 [1536], P('groups'), parts along dimension 0, may hold values from -6 to 6
- conv_kernel: bfloat16 [96, 1, 7, 7, 7], replicated, may hold values from -0.3125 to 0.3125
- conv_bias: float32 [96], replicated, may hold values from -4 to 4
- film_weight: bfloat16 [768, 192], replicated, may hold values from -0.21875 to 0.21875
- film_bias: float32 [192], replicated, may hold values from -3 to 3
- in_weight: bfloat16 [96, 384], replicated, may hold values from -0.625 to 0.625
- in_bias: float32 [384], replicated, may hold values from -3 to 3
- out_weight: bfloat16 [384, 96], replicated, may hold values from -0.3125 to 0.3125
Outputs:
- grad_input: bfloat16 [4, 16, 16, 3072], P('groups', 'depth', 'rows', 'cols'), parts along dimension 0
- grad_kernel: float32 [192, 1, 7, 7, 7], P('groups'), parts along dimension 0
- grad_conv_bias: float32 [192], P('groups'), parts along dimension 0
- grad_film: float32 [384], P('groups'), parts along dimension 0
- grad_in_weight: float32 [192, 384], P('groups'), parts along dimension 0
- grad_in_bias: float32 [768], P('groups'), parts along dimension 0
- grad_out_weight: float32 [768, 96], P('groups'), parts along dimension 0
There are 2 independent parts, one for each index of `groups`. A program takes and returns all parts, laid end to end along the dimension named above; an argument that names none is the same for every part. Nothing has to cross between parts.
All inputs are finite; a program needn't handle non-finite values.
Results may differ from a plain program's by a relative error of at most 0.0062.
Values may be sent and summed in bfloat16 or wider, within the bound.
A program may use at most 64 MiB of HBM per device.

v0:
```python
import math
import jax
import jax.numpy as jnp
from jax import lax
from jax.sharding import PartitionSpec as P

K = 7
epsilon = 1e-06
last_dims = ("NDHWC", "OIDHW", "NDHWC")
grad_dims = ("NDHWC", "DHWIO", "NDHWC")


def padded_2(block, sides, width):
    for axis, dim in sides:
        count = lax.axis_size(axis)
        forward = [(i, i + 1) for i in range(count - 1)]
        backward = [(target, source) for source, target in forward]
        low = lax.ppermute(
            lax.slice_in_dim(block, block.shape[dim] - width, None, axis=dim), axis, forward
        )
        high = lax.ppermute(lax.slice_in_dim(block, 0, width, axis=dim), axis, backward)
        block = jnp.concatenate([low, block, high], axis=dim)
    return block


def depthwise(padded, kernel):
    return lax.conv_general_dilated(
        padded,
        kernel,
        (1, 1, 1),
        "VALID",
        dimension_numbers=last_dims,
        feature_group_count=kernel.shape[0],
        preferred_element_type=jnp.float32,
    )


def widen(field):
    half_width = K // 2
    result = padded_2(field, (("depth", 1), ("rows", 2), ("cols", 3)), half_width)
    return result


def pointwise(conv_flat, grad_flat, film_vec, in_weight, in_bias, out_weight):
    channels = conv_flat.shape[0]
    chan_mean = jnp.mean(conv_flat, axis=0)
    centred = conv_flat - chan_mean
    variance = jnp.mean(centred * centred, axis=0)
    inverse = lax.rsqrt(variance + epsilon)
    normed = centred * inverse
    scale_vec = 1.0 + film_vec[:channels, None]
    hidden_in = (normed * scale_vec + film_vec[channels:, None]).astype(jnp.bfloat16)
    pre_act = jnp.dot(in_weight.T, hidden_in, preferred_element_type=jnp.float32) + in_bias[:, None]
    post_act, gelu_back = jax.vjp(jax.nn.gelu, pre_act)
    act_low = post_act.astype(jnp.bfloat16)
    grad_act = jnp.dot(out_weight, grad_flat, preferred_element_type=jnp.float32)
    grad_pre = gelu_back(grad_act)[0]
    grad_low = grad_pre.astype(jnp.bfloat16)
    grad_hidden = jnp.dot(in_weight, grad_low, preferred_element_type=jnp.float32)
    grad_out_w = jnp.dot(act_low, grad_flat.T, preferred_element_type=jnp.float32)
    grad_in_w = jnp.dot(hidden_in, grad_low.T, preferred_element_type=jnp.float32)
    grad_in_b = jnp.sum(grad_pre, axis=1)
    grad_film = jnp.concatenate(
        [jnp.sum(grad_hidden * normed, axis=1), jnp.sum(grad_hidden, axis=1)]
    )
    grad_normed = grad_hidden * scale_vec
    slope = (
        (
            grad_normed
            - jnp.mean(grad_normed, axis=0)
            - normed * jnp.mean(grad_normed * normed, axis=0)
        )
        * inverse
    ).astype(jnp.bfloat16)
    return (slope, (grad_in_w, grad_in_b, grad_out_w, grad_film))


def local(
    volume,
    grad_out,
    report,
    conv_kernel,
    conv_bias,
    film_weight,
    film_bias,
    in_weight,
    in_bias,
    out_weight,
):
    crops, slices, lines, merged = volume.shape
    channels = conv_kernel.shape[0]
    local_shape = (crops, slices, lines, merged // channels, channels)
    film_vec = (
        jnp.dot(report[None, :], film_weight, preferred_element_type=jnp.float32)[0] + film_bias
    )
    local_vol = volume.reshape(local_shape)
    local_grad = grad_out.reshape(local_shape)
    padded = widen(local_vol)
    conv_out = depthwise(padded, conv_kernel) + conv_bias
    conv_flat = conv_out.reshape(-1, channels).T
    grad_flat = local_grad.reshape(-1, channels).T
    slope_flat, local_grads = pointwise(
        conv_flat, grad_flat, film_vec, in_weight, in_bias, out_weight
    )
    voxel_count = (
        conv_flat.shape[1] * lax.axis_size("depth") * lax.axis_size("rows") * lax.axis_size("cols")
    )
    factor = 1.0 / math.sqrt(voxel_count)
    term_in_w = local_grads[0] * factor
    term_in_b = local_grads[1] * factor
    term_out_w = local_grads[2] * factor
    term_film = local_grads[3] * factor
    summed_mlp = lax.psum((term_in_w, term_in_b, term_out_w, term_film), ("depth", "rows", "cols"))
    slope_vol = slope_flat.T.reshape(local_shape)
    slope_pad = widen(slope_vol)
    flipped = conv_kernel[:, :, ::-1, ::-1, ::-1]
    grad_input = (
        (local_grad.astype(jnp.float32) + depthwise(slope_pad, flipped))
        .astype(jnp.bfloat16)
        .reshape(volume.shape)
    )
    kernel_local = jnp.zeros((1, K, K, K, channels), jnp.float32)
    for crop_index in range(crops):
        kernel_local = kernel_local + lax.conv_general_dilated(
            padded[crop_index][None],
            slope_vol[crop_index][:, :, :, None, :],
            (1, 1, 1),
            "VALID",
            dimension_numbers=grad_dims,
            feature_group_count=channels,
            preferred_element_type=jnp.float32,
        )
    term_kernel = jnp.moveaxis(kernel_local[0], 3, 0)[:, None] * factor
    term_bias = jnp.sum(slope_flat.astype(jnp.float32), axis=1) * factor
    summed_conv = lax.psum((term_kernel, term_bias), ("depth", "rows", "cols"))
    totals = tuple(summed_mlp) + tuple(summed_conv)
    return (grad_input, totals[4], totals[5], totals[3], totals[0], totals[1], totals[2])


def solution(mesh):
    in_specs = (
        P("groups", "depth", "rows", "cols"),
        P("groups", "depth", "rows", "cols"),
        P("groups"),
        P(),
        P(),
        P(),
        P(),
        P(),
        P(),
        P(),
    )
    out_specs = (
        P("groups", "depth", "rows", "cols"),
        P("groups", None, None, None, None),
        P("groups"),
        P("groups"),
        P("groups", None),
        P("groups"),
        P("groups", None),
    )
    return jax.shard_map(local, mesh=mesh, in_specs=in_specs, out_specs=out_specs, check_vma=False)
```

profile of v0, /device:TPU:8, one launch (start us, length us, event | category | flops | bytes accessed | tf_op | source)
XLA Modules:
  0.0 245.4 jit_solution(1171630249008193471)
XLA Ops:
  7.2 1.2 reshape.65
  8.8 3.5 %collective-permute-start = (bf16[2,3,8,16,96]{4,0,3,2,1:T(2,128)(2,1)S(1)}, bf16[2,3,8,16,96]{4,0,3,2,1:T(2,128)(2,1)S(1)}, u32[]{:S(2)}, u32[]{:S(2)}) collective-permute-start(bf16[2,3,8,16,96]{4,0,3,2,1:T(2,128)(2,1)S(1)} %copy.119), channel_id=1, source_target_pairs={{0,4},{4,8},{8,12},{1,5},{5,9},{9,13},{2,6},{6,10},{10,14},{3,7},{... | collective-permute-start | bytes 442376 | tf_op jit(solution)/shard_map/ppermute | solution.py:18
  12.5 2.4 collective-permute-start.1
  14.8 0.2 reshape_reshape.3
  15.3 2.0 collective-permute-done
  17.4 0.3 constant_dynamic-update-slice_fusion.1
  17.7 3.0 %collective-permute-done.1 = bf16[2,3,8,16,96]{4,0,3,2,1:T(2,128)(2,1)S(1)} collective-permute-done((bf16[2,3,8,16,96]{4,0,3,2,1:T(2,128)(2,1)S(1)}, bf16[2,3,8,16,96]{4,0,3,2,1:T(2,128)(2,1)S(1)}, u32[]{:S(2)}, u32[]{:S(2)}) %collective-permute-start.1) | collective-permute-done | bytes 147488 | tf_op jit(solution)/shard_map/ppermute | solution.py:21
  20.9 0.4 fusion.54
  21.2 3.4 %collective-permute-start.2 = (bf16[2,10,3,16,96]{4,0,3,2,1:T(2,128)(2,1)S(1)}, bf16[2,10,3,16,96]{4,0,3,2,1:T(2,128)(2,1)S(1)}, u32[]{:S(2)}, u32[]{:S(2)}) collective-permute-start(bf16[2,10,3,16,96]{4,0,3,2,1:T(2,128)(2,1)S(1)} %get-tuple-element.57), channel_id=1, source_target_pairs={{0,2},{1,3},{4,6},{5,7},{8,10},{9,11},{12,14},{13,15},{16,18},{17,... | collective-permute-start | bytes 552968 | tf_op jit(solution)/shard_map/ppermute | solution.py:18
  24.7 1.3 collective-permute-start.3
  26.1 2.6 %collective-permute-done.2 = bf16[2,10,3,16,96]{4,0,3,2,1:T(2,128)(2,1)S(1)} collective-permute-done((bf16[2,10,3,16,96]{4,0,3,2,1:T(2,128)(2,1)S(1)}, bf16[2,10,3,16,96]{4,0,3,2,1:T(2,128)(2,1)S(1)}, u32[]{:S(2)}, u32[]{:S(2)}) %collective-permute-start.2) | collective-permute-done | bytes 184352 | tf_op jit(solution)/shard_map/ppermute | solution.py:18
  28.7 4.1 %collective-permute-done.3 = bf16[2,10,3,16,96]{4,0,3,2,1:T(2,128)(2,1)S(1)} collective-permute-done((bf16[2,10,3,16,96]{4,0,3,2,1:T(2,128)(2,1)S(1)}, bf16[2,10,3,16,96]{4,0,3,2,1:T(2,128)(2,1)S(1)}, u32[]{:S(2)}, u32[]{:S(2)}) %collective-permute-start.3) | collective-permute-done | bytes 184352 | tf_op jit(solution)/shard_map/ppermute | solution.py:21
  32.8 0.7 pad_maximum_fusion.6
  33.5 1.3 collective-permute-start.4
  34.9 1.5 collective-permute-start.5
  36.5 1.8 collective-permute-done.5
  38.2 7.8 %pad_maximum_fusion = bf16[2,10,14,22,96]{4,0,3,2,1:T(2,128)(2,1)S(1)} fusion(bf16[2,10,14,3,96]{4,0,3,2,1:T(2,128)(2,1)S(1)} %collective-permute-done.5, bf16[2,10,3,16,96]{4,0,3,2,1:T(2,128)(2,1)S(1)} %collective-permute-done.3, bf16[2,10,8,16,96]{4,0,3,2,1:T(2,128)(2,1)S(1)} %constant_dynamic-update-slice_fusion, ...), kind=kLoop, calls=%fused_computation.6 | loop fusion | flops 2365440 | bytes 2365440 | tf_op jit(solution)/shard_map/concatenate | solution.py:22
  46.0 19.1 %fusion.59 = (f32[2,4,8,16]{0,3,2,1:T(8,128)S(1)}, f32[2,4,8,16,96]{4,0,3,2,1:T(2,128)S(1)}) fusion(f32[96]{0:T(128)S(1)} %copy-done.13, bf16[2,10,14,22,96]{4,0,3,2,1:T(2,128)(2,1)S(1)} %pad_maximum_fusion, bf16[96,1,7,7,7]{0,4,3,2,1:T(8,128)(2,1)S(1)} %copy-done.10), kind=kOutput, calls=%fused_computation.92 | convolution fusion | flops 67632128 | bytes 1646272 | tf_op jit(solution)/shard_map/conv_general_dilated | solution.py:27
  65.4 0.3 copy.89
  66.0 0.5 convolution_add_fusion
  66.5 1.3 convolution_multiply_fusion.1
  67.8 1.3 fusion.60
  69.2 0.4 fusion.31
  70.1 15.6 %fusion = f32[1,7,7,7,96]{4,0,3,2,1:T(1,128)S(1)} fusion(bf16[2,10,14,22,96]{4,0,3,2,1:T(2,128)(2,1)} %copy-done.1, bf16[4,8,16,1,96]{4,2,1,0,3:T(8,128)(2,1)S(1)} %bitcast.90), kind=kOutput, calls=%fused_computation.2 | convolution fusion | flops 33718272 | bytes 1412736 | tf_op jit(solution)/shard_map/conv_general_dilated | solution.py:124
  85.8 0.2 copy.121
  86.0 3.6 %collective-permute-start.6 = (bf16[2,3,8,16,96]{4,0,3,2,1:T(2,128)(2,1)S(1)}, bf16[2,3,8,16,96]{4,0,3,2,1:T(2,128)(2,1)S(1)}, u32[]{:S(2)}, u32[]{:S(2)}) collective-permute-start(bf16[2,3,8,16,96]{4,0,3,2,1:T(2,128)(2,1)S(1)} %copy.121), channel_id=1, source_target_pairs={{0,4},{4,8},{8,12},{1,5},{5,9},{9,13},{2,6},{6,10},{10,14},{3,7},{... | collective-permute-start | bytes 442376 | tf_op jit(solution)/shard_map/ppermute | solution.py:18
  89.9 2.4 collective-permute-start.7
  92.3 13.7 %fusion.26 = f32[1,7,7,7,96]{4,0,3,2,1:T(1,128)S(1)} fusion(f32[1,7,7,7,96]{4,0,3,2,1:T(1,128)S(1)} %fusion, bf16[2,10,14,22,96]{4,0,3,2,1:T(2,128)(2,1)S(1)} %copy-done.2, bf16[4,8,16,1,96]{4,2,1,0,3:T(8,128)(2,1)S(1)} %bitcast.89), kind=kOutput, calls=%fused_computation.33 | convolution fusion | flops 33784128 | bytes 1544448 | tf_op jit(solution)/shard_map/conv_general_dilated | solution.py:124
  106.0 1.1 convolution_multiply_fusion
  107.2 0.3 constant_dynamic-update-slice_fusion.4
  107.7 0.4 fusion.53
  108.0 1.5 collective-permute-start.8
  109.5 1.3 collective-permute-start.9
  110.8 0.7 copy.128
  111.5 0.2 convert_reduce_fusion
  111.8 2.8 %collective-permute-done.8 = bf16[2,10,3,16,96]{4,0,3,2,1:T(2,128)(2,1)S(1)} collective-permute-done((bf16[2,10,3,16,96]{4,0,3,2,1:T(2,128)(2,1)S(1)}, bf16[2,10,3,16,96]{4,0,3,2,1:T(2,128)(2,1)S(1)}, u32[]{:S(2)}, u32[]{:S(2)}) %collective-permute-start.8) | collective-permute-done | bytes 184352 | tf_op jit(solution)/shard_map/ppermute | solution.py:18
  114.5 4.1 %collective-permute-done.9 = bf16[2,10,3,16,96]{4,0,3,2,1:T(2,128)(2,1)S(1)} collective-permute-done((bf16[2,10,3,16,96]{4,0,3,2,1:T(2,128)(2,1)S(1)}, bf16[2,10,3,16,96]{4,0,3,2,1:T(2,128)(2,1)S(1)}, u32[]{:S(2)}, u32[]{:S(2)}) %collective-permute-start.9) | collective-permute-done | bytes 184352 | tf_op jit(solution)/shard_map/ppermute | solution.py:21
  118.7 0.7 pad_maximum_fusion.3
  119.4 1.3 collective-permute-start.10
  120.7 1.3 collective-permute-start.11
  122.1 24.1 %all-reduce = (f32[96]{0:T(128)}, f32[192]{0:T(256)}, f32[384]{0:T(512)}) all-reduce(f32[96]{0:T(128)S(1)} %broadcast_multiply_fusion.4, f32[192]{0:T(256)S(1)} %maximum_multiply_fusion, f32[384]{0:T(512)S(1)} %broadcast_multiply_fusion.3), channel_id=1, replica_groups=mesh['groups'=2,'depth'=4,'rows'=2,'cols'=2] {'depth','rows','cols'}, use_global_device_ids=true, to_apply=%region_6.0 | all-reduce | flops 672 | bytes 5376 | tf_op jit(solution)/shard_map/psum | solution.py:135
  146.2 59.3 %all-reduce.4.cloned.1.call-done = (f32[96,1,7,7,7]{0,4,3,2,1:T(8,128)}, f32[96,384]{1,0:T(8,128)}, f32[384,96]{0,1:T(8,128)}) async-done(((f32[96,1,7,7,7]{0,4,3,2,1:T(8,128)}, f32[96,384]{1,0:T(8,128)}, f32[384,96]{0,1:T(8,128)}), (f32[96,1,7,7,7]{0,4,3,2,1:T(8,128)}, f32[96,384]{1,0:T(8,128)}, f32[384,96]{0,1:T(8,128)})) %all-reduce.4.cloned.1.call-update) | async-done | bytes 426640 | tf_op jit(solution)/shard_map/psum | solution.py:135
  205.5 1.8 copy.102
  207.3 7.8 %fusion.81 = bf16[2,10,14,22,96]{4,0,3,2,1:T(2,128)(2,1)S(1)} fusion(bf16[2,10,14,3,96]{4,0,3,2,1:T(2,128)(2,1)S(1)} %collective-permute-done.11, bf16[2,10,3,16,96]{4,0,3,2,1:T(2,128)(2,1)S(1)} %collective-permute-done.9, bf16[2,10,8,16,96]{4,0,3,2,1:T(2,128)(2,1)S(1)} %constant_dynamic-update-slice_fusion.3, ...), kind=kLoop, calls=%fused_computation.8.clone.1 | loop fusion | flops 2365440 | bytes 2365440 | tf_op jit(solution)/shard_map/conv_general_dilated | solution.py:27
  215.1 20.6 %fusion.4 = f32[2,4,8,16,96]{4,0,3,2,1:T(2,128)S(1)} fusion(bf16[96,1,7,7,7]{0,4,3,2,1:T(8,128)(2,1)S(1)} %copy-done.11, bf16[2,10,14,22,96]{4,0,3,2,1:T(2,128)(2,1)S(1)} %fusion.81), kind=kOutput, calls=%fused_computation.7 | convolution fusion | flops 67436544 | bytes 1641792 | tf_op jit(solution)/shard_map/conv_general_dilated | solution.py:27
  235.9 0.9 reshape.68
  236.8 0.7 copy.136
  237.5 0.7 copy.137
  (65 shorter events, 3.1 us)
Async XLA Ops:
  7.2 18.8 %copy-start = (bf16[768,192]{0,1:T(8,128)(2,1)S(1)}, bf16[768,192]{0,1:T(8,128)(2,1)}, u32[]{:S(2)}) copy-start(bf16[768,192]{0,1:T(8,128)(2,1)} %param.15) | copy-start | bytes 884740
  7.2 7.6 %copy-start.3 = (bf16[2,4,8,1536]{3,2,1,0:T(8,128)(2,1)S(1)}, bf16[2,4,8,1536]{3,2,1,0:T(8,128)(2,1)}, u32[]{:S(2)}) copy-start(bf16[2,4,8,1536]{3,2,1,0:T(8,128)(2,1)} %param.11) | copy-start | bytes 589828
  7.2 8.1 %copy-start.7 = (bf16[768]{0:T(1024)(128)(2,1)S(1)}, bf16[768]{0:T(1024)(128)(2,1)}, u32[]{:S(2)}) copy-start(bf16[768]{0:T(1024)(128)(2,1)} %param.12) | copy-start | bytes 4612
  7.2 198.3 %all-reduce.4.cloned.1.call-start = ((), (), s32[]{:S(2)}) async-start(), calls=%async_computation | async-start | bytes 991232 | tf_op jit(solution)/shard_map/psum | solution.py:135
  8.8 8.5 %collective-permute-start = (bf16[2,3,8,16,96]{4,0,3,2,1:T(2,128)(2,1)S(1)}, bf16[2,3,8,16,96]{4,0,3,2,1:T(2,128)(2,1)S(1)}, u32[]{:S(2)}, u32[]{:S(2)}) collective-permute-start(bf16[2,3,8,16,96]{4,0,3,2,1:T(2,128)(2,1)S(1)} %copy.119), channel_id=1, source_target_pairs={{0,4},{4,8},{8,12},{1,5},{5,9},{9,13},{2,6},{6,10},{10,14},{3,7},{... | collective-permute-start | bytes 442376 | tf_op jit(solution)/shard_map/ppermute | solution.py:18
  12.5 8.3 %collective-permute-start.1 = (bf16[2,3,8,16,96]{4,0,3,2,1:T(2,128)(2,1)S(1)}, bf16[2,3,8,16,96]{4,0,3,2,1:T(2,128)(2,1)S(1)}, u32[]{:S(2)}, u32[]{:S(2)}) collective-permute-start(bf16[2,3,8,16,96]{4,0,3,2,1:T(2,128)(2,1)S(1)} %copy.120), channel_id=1, source_target_pairs={{4,0},{8,4},{12,8},{5,1},{9,5},{13,9},{6,2},{10,6},{14,10},{7,3},{... | collective-permute-start | bytes 442376 | tf_op jit(solution)/shard_map/ppermute | solution.py:21
  15.1 11.0 %copy-start.9 = (f32[192]{0:T(256)S(1)}, f32[192]{0:T(256)}, u32[]{:S(2)}) copy-start(f32[192]{0:T(256)} %param.16) | copy-start | bytes 2308
  21.2 7.5 %collective-permute-start.2 = (bf16[2,10,3,16,96]{4,0,3,2,1:T(2,128)(2,1)S(1)}, bf16[2,10,3,16,96]{4,0,3,2,1:T(2,128)(2,1)S(1)}, u32[]{:S(2)}, u32[]{:S(2)}) collective-permute-start(bf16[2,10,3,16,96]{4,0,3,2,1:T(2,128)(2,1)S(1)} %get-tuple-element.57), channel_id=1, source_target_pairs={{0,2},{1,3},{4,6},{5,7},{8,10},{9,11},{12,14},{13,15},{16,18},{17,... | collective-permute-start | bytes 552968 | tf_op jit(solution)/shard_map/ppermute | solution.py:18
  24.7 8.2 %collective-permute-start.3 = (bf16[2,10,3,16,96]{4,0,3,2,1:T(2,128)(2,1)S(1)}, bf16[2,10,3,16,96]{4,0,3,2,1:T(2,128)(2,1)S(1)}, u32[]{:S(2)}, u32[]{:S(2)}) collective-permute-start(bf16[2,10,3,16,96]{4,0,3,2,1:T(2,128)(2,1)S(1)} %get-tuple-element.58), channel_id=1, source_target_pairs={{2,0},{3,1},{6,4},{7,5},{10,8},{11,9},{14,12},{15,13},{18,16},{19,... | collective-permute-start | bytes 552968 | tf_op jit(solution)/shard_map/ppermute | solution.py:21
  33.5 2.9 %collective-permute-start.4 = (bf16[2,10,14,3,96]{4,0,3,2,1:T(2,128)(2,1)S(1)}, bf16[2,10,14,3,96]{4,0,3,2,1:T(2,128)(2,1)S(1)}, u32[]{:S(2)}, u32[]{:S(2)}) collective-permute-start(bf16[2,10,14,3,96]{4,0,3,2,1:T(2,128)(2,1)S(1)} %get-tuple-element.53), channel_id=1, source_target_pairs={{0,1},{2,3},{4,5},{6,7},{8,9},{10,11},{12,13},{14,15},{16,17},{18,... | collective-permute-start | bytes 483848 | tf_op jit(solution)/shard_map/ppermute | solution.py:18
  34.9 3.4 %collective-permute-start.5 = (bf16[2,10,14,3,96]{4,0,3,2,1:T(2,128)(2,1)S(1)}, bf16[2,10,14,3,96]{4,0,3,2,1:T(2,128)(2,1)S(1)}, u32[]{:S(2)}, u32[]{:S(2)}) collective-permute-start(bf16[2,10,14,3,96]{4,0,3,2,1:T(2,128)(2,1)S(1)} %get-tuple-element.54), channel_id=1, source_target_pairs={{1,0},{3,2},{5,4},{7,6},{9,8},{11,10},{13,12},{15,14},{17,16},{19,... | collective-permute-start | bytes 483848 | tf_op jit(solution)/shard_map/ppermute | solution.py:21
  36.4 9.5 %copy-start.10 = (bf16[96,1,7,7,7]{0,4,3,2,1:T(8,128)(2,1)S(1)}, bf16[96,1,7,7,7]{0,4,3,2,1:T(8,128)(2,1)}, u32[]{:S(2)}) copy-start(bf16[96,1,7,7,7]{0,4,3,2,1:T(8,128)(2,1)} %param.13) | copy-start | bytes 197572
  36.5 9.6 %copy-start.13 = (f32[96]{0:T(128)S(1)}, f32[96]{0:T(128)}, u32[]{:S(2)}) copy-start(f32[96]{0:T(128)} %param.14) | copy-start | bytes 1156
  46.0 19.1 %copy-start.1 = (bf16[2,10,14,22,96]{4,0,3,2,1:T(2,128)(2,1)}, bf16[2,10,14,22,96]{4,0,3,2,1:T(2,128)(2,1)S(1)}, u32[]{:S(2)}) copy-start(bf16[2,10,14,22,96]{4,0,3,2,1:T(2,128)(2,1)S(1)} %pad_maximum_fusion) | copy-start | bytes 3548164
  65.1 0.9 copy-start.4
  65.1 0.9 copy-start.8
  66.5 1.4 copy-start.12
  85.8 6.5 %copy-start.2 = (bf16[2,10,14,22,96]{4,0,3,2,1:T(2,128)(2,1)S(1)}, bf16[2,10,14,22,96]{4,0,3,2,1:T(2,128)(2,1)}, u32[]{:S(2)}) copy-start(bf16[2,10,14,22,96]{4,0,3,2,1:T(2,128)(2,1)} %copy-done.1) | copy-start | bytes 3548164
  86.0 21.0 %collective-permute-start.6 = (bf16[2,3,8,16,96]{4,0,3,2,1:T(2,128)(2,1)S(1)}, bf16[2,3,8,16,96]{4,0,3,2,1:T(2,128)(2,1)S(1)}, u32[]{:S(2)}, u32[]{:S(2)}) collective-permute-start(bf16[2,3,8,16,96]{4,0,3,2,1:T(2,128)(2,1)S(1)} %copy.121), channel_id=1, source_target_pairs={{0,4},{4,8},{8,12},{1,5},{5,9},{9,13},{2,6},{6,10},{10,14},{3,7},{... | collective-permute-start | bytes 442376 | tf_op jit(solution)/shard_map/ppermute | solution.py:18
  89.9 17.6 %collective-permute-start.7 = (bf16[2,3,8,16,96]{4,0,3,2,1:T(2,128)(2,1)S(1)}, bf16[2,3,8,16,96]{4,0,3,2,1:T(2,128)(2,1)S(1)}, u32[]{:S(2)}, u32[]{:S(2)}) collective-permute-start(bf16[2,3,8,16,96]{4,0,3,2,1:T(2,128)(2,1)S(1)} %copy.122), channel_id=1, source_target_pairs={{4,0},{8,4},{12,8},{5,1},{9,5},{13,9},{6,2},{10,6},{14,10},{7,3},{... | collective-permute-start | bytes 442376 | tf_op jit(solution)/shard_map/ppermute | solution.py:21
  108.0 6.5 %collective-permute-start.8 = (bf16[2,10,3,16,96]{4,0,3,2,1:T(2,128)(2,1)S(1)}, bf16[2,10,3,16,96]{4,0,3,2,1:T(2,128)(2,1)S(1)}, u32[]{:S(2)}, u32[]{:S(2)}) collective-permute-start(bf16[2,10,3,16,96]{4,0,3,2,1:T(2,128)(2,1)S(1)} %get-tuple-element.55), channel_id=1, source_target_pairs={{0,2},{1,3},{4,6},{5,7},{8,10},{9,11},{12,14},{13,15},{16,18},{17,... | collective-permute-start | bytes 552968 | tf_op jit(solution)/shard_map/ppermute | solution.py:18
  109.5 9.2 %collective-permute-start.9 = (bf16[2,10,3,16,96]{4,0,3,2,1:T(2,128)(2,1)S(1)}, bf16[2,10,3,16,96]{4,0,3,2,1:T(2,128)(2,1)S(1)}, u32[]{:S(2)}, u32[]{:S(2)}) collective-permute-start(bf16[2,10,3,16,96]{4,0,3,2,1:T(2,128)(2,1)S(1)} %get-tuple-element.56), channel_id=1, source_target_pairs={{2,0},{3,1},{6,4},{7,5},{10,8},{11,9},{14,12},{15,13},{18,16},{19,... | collective-permute-start | bytes 552968 | tf_op jit(solution)/shard_map/ppermute | solution.py:21
  119.4 87.9 %collective-permute-start.10 = (bf16[2,10,14,3,96]{4,0,3,2,1:T(2,128)(2,1)S(1)}, bf16[2,10,14,3,96]{4,0,3,2,1:T(2,128)(2,1)S(1)}, u32[]{:S(2)}, u32[]{:S(2)}) collective-permute-start(bf16[2,10,14,3,96]{4,0,3,2,1:T(2,128)(2,1)S(1)} %get-tuple-element.51), channel_id=1, source_target_pairs={{0,1},{2,3},{4,5},{6,7},{8,9},{10,11},{12,13},{14,15},{16,17},{18,... | collective-permute-start | bytes 483848 | tf_op jit(solution)/shard_map/ppermute | solution.py:18
  120.7 86.6 %collective-permute-start.11 = (bf16[2,10,14,3,96]{4,0,3,2,1:T(2,128)(2,1)S(1)}, bf16[2,10,14,3,96]{4,0,3,2,1:T(2,128)(2,1)S(1)}, u32[]{:S(2)}, u32[]{:S(2)}) collective-permute-start(bf16[2,10,14,3,96]{4,0,3,2,1:T(2,128)(2,1)S(1)} %get-tuple-element.52), channel_id=1, source_target_pairs={{1,0},{3,2},{5,4},{7,6},{9,8},{11,10},{13,12},{15,14},{17,16},{19,... | collective-permute-start | bytes 483848 | tf_op jit(solution)/shard_map/ppermute | solution.py:21
  207.3 7.8 %copy-start.11 = (bf16[96,1,7,7,7]{0,4,3,2,1:T(8,128)(2,1)S(1)}, bf16[96,1,7,7,7]{0,4,3,2,1:T(8,128)(2,1)}, u32[]{:S(2)}) copy-start(bf16[96,1,7,7,7]{0,4,3,2,1:T(8,128)(2,1)} %param.13) | copy-start | bytes 197572
  235.8 1.0 copy-start.6
  235.8 1.7 copy-start.5
Sparse Core Ops, SparseCore 0:
  111.7 93.8 all-reduce.3
where the time goes:
time: 249 us; the launch traced here: 245 us
  waiting for transfers between devices  79.6 us (32%)
  matrix products  73.7 us (30%)
  starting transfers between devices  24.7 us (10%)
  blocking collectives  24.1 us (10%)
  other arithmetic  17.7 us (7%)
  between operations  15 us (6%)
  local copies, waits for them, and re-layouts  10.4 us (4%)
    psum x1, waiting for transfers between devices, local(): summed_conv = lax.psum((term_kernel, term_bias), ('depth', 'rows', 'cols'))  59.3 us
    conv_general_dilated x2, matrix products, depthwise(): lax.conv_general_dilated(padded, kernel, (1, 1, 1), 'VALID', dimension_nu...  39.7 us
    conv_general_dilated x2, matrix products, local(): lax.conv_general_dilated(padded[crop_index][None], slope_vol[crop_index][...  29.3 us
    psum x1, blocking collectives, local(): summed_conv = lax.psum((term_kernel, term_bias), ('depth', 'rows', 'cols'))  24.1 us
    ppermute x6, starting transfers between devices, padded_2(): lax.ppermute(lax.slice_in_dim(block, block.shape[dim] - width, None, axis...  14.6 us
    ppermute x6, waiting for transfers between devices, padded_2(): lax.ppermute(lax.slice_in_dim(block, 0, width, axis=dim), axis, backward)  13 us
    ppermute x6, starting transfers between devices, padded_2(): lax.ppermute(lax.slice_in_dim(block, 0, width, axis=dim), axis, backward)  10.1 us
    conv_general_dilated x1, other arithmetic, depthwise(): lax.conv_general_dilated(padded, kernel, (1, 1, 1), 'VALID', dimension_nu...  7.79 us
  transfers between devices with their start and end apart: 13, of which 8 were waited for; matrix products, arithmetic and copies ran while one was open for 8% of the time, Pallas kernels for 0%

commit v1 on v0

--- a/solution.py
+++ b/solution.py
@@ -3,6 +3,7 @@
 import jax.numpy as jnp
 from jax import lax
 from jax.sharding import PartitionSpec as P
+from jax.lax import psum
 
 K = 7
 epsilon = 1e-06
@@ -132,7 +133,9 @@
         )
     term_kernel = jnp.moveaxis(kernel_local[0], 3, 0)[:, None] * factor
     term_bias = jnp.sum(slope_flat.astype(jnp.float32), axis=1) * factor
-    summed_conv = lax.psum((term_kernel, term_bias), ("depth", "rows", "cols"))
+    summed_conv = (term_kernel, term_bias)
+    for dd in (("rows", "cols"), "depth"):
+        summed_conv = psum(summed_conv, dd)
     totals = tuple(summed_mlp) + tuple(summed_conv)
     return (grad_input, totals[4], totals[5], totals[3], totals[0], totals[1], totals[2])
 

time: 249 us -> 298 us (1.20)
  waiting for transfers between devices: 79.6 us -> 101 us
  blocking collectives: 24.1 us -> 41.9 us
  local copies, waits for them, and re-layouts: 10.4 us -> 14.7 us
    psum x1 -> x3, waiting for transfers between devices: 59.3 us -> 87.2 us  [the longest x1 56 us: local(): lax.psum((term_in_w, term_in_b, term_out_w, term_film), ('depth', 'rows',...]
    psum x1 -> x3, blocking collectives: 24.1 us -> 41.9 us  [the longest x1 25 us: local(): lax.psum((term_in_w, term_in_b, term_out_w, term_film), ('depth', 'rows',...]
    ppermute x6, waiting for transfers between devices: 13 us -> 8.85 us  [padded_2(): lax.ppermute(lax.slice_in_dim(block, 0, width, axis=dim), axis, backward)]
    unnamed x41 -> x39, local copies, waits for them, and re-layouts: 5.73 us -> 8.5 us
  transfers between devices with their start and end apart: 13 -> 15, of which waited for: 8 -> 7; matrix products, arithmetic and copies ran while one was open for 8% -> 18% of each run, Pallas kernels for 0% -> 0%
where the time goes in v1:
time: 298 us; the launch traced here: 292 us
  waiting for transfers between devices  101 us (34%)
  matrix products  76.5 us (26%)
  blocking collectives  41.9 us (14%)
  starting transfers between devices  26.3 us (9%)
  other arithmetic  17.7 us (6%)
  local copies, waits for them, and re-layouts  14.7 us (5%)
  between operations  14.5 us (5%)
    psum x1, waiting for transfers between devices, local(): lax.psum((term_in_w, term_in_b, term_out_w, term_film), ('depth', 'rows',...  56 us
    conv_general_dilated x2, matrix products, depthwise(): lax.conv_general_dilated(padded, kernel, (1, 1, 1), 'VALID', dimension_nu...  40.2 us
    conv_general_dilated x2, matrix products, local(): lax.conv_general_dilated(padded[crop_index][None], slope_vol[crop_index][...  31.6 us
    psum x2, waiting for transfers between devices, local(): summed_conv = psum(summed_conv, dd)  31.3 us
    psum x1, blocking collectives, local(): lax.psum((term_in_w, term_in_b, term_out_w, term_film), ('depth', 'rows',...  25 us
    psum x2, blocking collectives, local(): summed_conv = psum(summed_conv, dd)  17 us
    ppermute x6, starting transfers between devices, padded_2(): lax.ppermute(lax.slice_in_dim(block, block.shape[dim] - width, None, axis...  15.4 us
    ppermute x6, starting transfers between devices, padded_2(): lax.ppermute(lax.slice_in_dim(block, 0, width, axis=dim), axis, backward)  10.8 us
  transfers between devices with their start and end apart: 15, of which 7 were waited for; matrix products, arithmetic and copies ran while one was open for 18% of the time, Pallas kernels for 0%

profile of v1, /device:TPU:8, one launch (start us, length us, event | category | flops | bytes accessed | tf_op | source)
XLA Modules:
  0.0 292.4 jit_solution(16986937348938562531)
XLA Ops:
  7.2 1.2 reshape.65
  8.7 3.5 %collective-permute-start = (bf16[2,3,8,16,96]{4,0,3,2,1:T(2,128)(2,1)S(1)}, bf16[2,3,8,16,96]{4,0,3,2,1:T(2,128)(2,1)S(1)}, u32[]{:S(2)}, u32[]{:S(2)}) collective-permute-start(bf16[2,3,8,16,96]{4,0,3,2,1:T(2,128)(2,1)S(1)} %copy.119), channel_id=1, source_target_pairs={{0,4},{4,8},{8,12},{1,5},{5,9},{9,13},{2,6},{6,10},{10,14},{3,7},{... | collective-permute-start | bytes 442376 | tf_op jit(solution)/shard_map/ppermute | solution.py:19
  12.5 2.4 collective-permute-start.1
  15.3 2.0 collective-permute-done
  17.4 0.3 constant_dynamic-update-slice_fusion.1
  17.7 3.0 %collective-permute-done.1 = bf16[2,3,8,16,96]{4,0,3,2,1:T(2,128)(2,1)S(1)} collective-permute-done((bf16[2,3,8,16,96]{4,0,3,2,1:T(2,128)(2,1)S(1)}, bf16[2,3,8,16,96]{4,0,3,2,1:T(2,128)(2,1)S(1)}, u32[]{:S(2)}, u32[]{:S(2)}) %collective-permute-start.1) | collective-permute-done | bytes 147488 | tf_op jit(solution)/shard_map/ppermute | solution.py:22
  20.9 0.3 fusion.54
  21.2 3.4 %collective-permute-start.2 = (bf16[2,10,3,16,96]{4,0,3,2,1:T(2,128)(2,1)S(1)}, bf16[2,10,3,16,96]{4,0,3,2,1:T(2,128)(2,1)S(1)}, u32[]{:S(2)}, u32[]{:S(2)}) collective-permute-start(bf16[2,10,3,16,96]{4,0,3,2,1:T(2,128)(2,1)S(1)} %get-tuple-element.55), channel_id=1, source_target_pairs={{0,2},{1,3},{4,6},{5,7},{8,10},{9,11},{12,14},{13,15},{16,18},{17,... | collective-permute-start | bytes 552968 | tf_op jit(solution)/shard_map/ppermute | solution.py:19
  24.6 1.3 collective-permute-start.3
  26.1 2.6 collective-permute-done.2
  28.7 4.1 %collective-permute-done.3 = bf16[2,10,3,16,96]{4,0,3,2,1:T(2,128)(2,1)S(1)} collective-permute-done((bf16[2,10,3,16,96]{4,0,3,2,1:T(2,128)(2,1)S(1)}, bf16[2,10,3,16,96]{4,0,3,2,1:T(2,128)(2,1)S(1)}, u32[]{:S(2)}, u32[]{:S(2)}) %collective-permute-start.3) | collective-permute-done | bytes 184352 | tf_op jit(solution)/shard_map/ppermute | solution.py:22
  32.8 0.7 pad_maximum_fusion.6
  33.5 1.3 collective-permute-start.4
  34.8 1.5 collective-permute-start.5
  36.5 1.7 collective-permute-done.5
  38.2 7.8 %pad_maximum_fusion = bf16[2,10,14,22,96]{4,0,3,2,1:T(2,128)(2,1)S(1)} fusion(bf16[2,10,14,3,96]{4,0,3,2,1:T(2,128)(2,1)S(1)} %collective-permute-done.5, bf16[2,10,3,16,96]{4,0,3,2,1:T(2,128)(2,1)S(1)} %collective-permute-done.3, bf16[2,10,8,16,96]{4,0,3,2,1:T(2,128)(2,1)S(1)} %constant_dynamic-update-slice_fusion, ...), kind=kLoop, calls=%fused_computation.6 | loop fusion | flops 2365440 | bytes 2365440 | tf_op jit(solution)/shard_map/concatenate | solution.py:23
  46.0 19.1 %fusion.59 = (f32[2,4,8,16]{0,3,2,1:T(8,128)S(1)}, f32[2,4,8,16,96]{4,0,3,2,1:T(2,128)S(1)}) fusion(f32[96]{0:T(128)S(1)} %copy-done.12, bf16[2,10,14,22,96]{4,0,3,2,1:T(2,128)(2,1)S(1)} %pad_maximum_fusion, bf16[96,1,7,7,7]{0,4,3,2,1:T(8,128)(2,1)S(1)} %copy-done.9), kind=kOutput, calls=%fused_computation.92 | convolution fusion | flops 67632128 | bytes 1646272 | tf_op jit(solution)/shard_map/conv_general_dilated | solution.py:28
  66.0 0.4 convolution_add_fusion
  66.5 1.3 convolution_multiply_fusion.1
  67.8 1.3 fusion.60
  69.2 0.4 fusion.31
  70.1 16.3 %fusion = f32[1,7,7,7,96]{4,0,3,2,1:T(1,128)} fusion(bf16[2,10,14,22,96]{4,0,3,2,1:T(2,128)(2,1)} %copy-done.1, bf16[4,8,16,1,96]{4,2,1,0,3:T(8,128)(2,1)S(1)} %bitcast.90), kind=kOutput, calls=%fused_computation.2 | convolution fusion | flops 33718272 | bytes 1412736 | tf_op jit(solution)/shard_map/conv_general_dilated | solution.py:125
  86.3 0.8 copy.98
  87.3 3.6 %collective-permute-start.6 = (bf16[2,3,8,16,96]{4,0,3,2,1:T(2,128)(2,1)S(1)}, bf16[2,3,8,16,96]{4,0,3,2,1:T(2,128)(2,1)}, u32[]{:S(2)}, u32[]{:S(2)}) collective-permute-start(bf16[2,3,8,16,96]{4,0,3,2,1:T(2,128)(2,1)S(1)} %copy.121), channel_id=1, source_target_pairs={{0,4},{4,8},{8,12},{1,5},{5,9},{9,13},{2,6},{6,10},{10,14},{3,7},{... | collective-permute-start | bytes 442376 | tf_op jit(solution)/shard_map/ppermute | solution.py:19
  91.2 3.0 %collective-permute-start.7 = (bf16[2,3,8,16,96]{4,0,3,2,1:T(2,128)(2,1)S(1)}, bf16[2,3,8,16,96]{4,0,3,2,1:T(2,128)(2,1)}, u32[]{:S(2)}, u32[]{:S(2)}) collective-permute-start(bf16[2,3,8,16,96]{4,0,3,2,1:T(2,128)(2,1)S(1)} %copy.122), channel_id=1, source_target_pairs={{4,0},{8,4},{12,8},{5,1},{9,5},{13,9},{6,2},{10,6},{14,10},{7,3},{... | collective-permute-start | bytes 442376 | tf_op jit(solution)/shard_map/ppermute | solution.py:22
  94.2 15.4 %fusion.26 = f32[1,7,7,7,96]{4,0,3,2,1:T(1,128)} fusion(f32[1,7,7,7,96]{4,0,3,2,1:T(1,128)} %fusion, bf16[2,10,14,22,96]{4,0,3,2,1:T(2,128)(2,1)S(1)} %copy-done.2, bf16[4,8,16,1,96]{4,2,1,0,3:T(8,128)(2,1)} %bitcast.89), kind=kOutput, calls=%fused_computation.33 | convolution fusion | flops 33784128 | bytes 1544448 | tf_op jit(solution)/shard_map/conv_general_dilated | solution.py:125
  109.6 1.1 convolution_multiply_fusion
  110.7 1.1 constant_dynamic-update-slice_fusion.5
  111.8 0.3 constant_dynamic-update-slice_fusion.4
  112.1 1.1 constant_dynamic-update-slice_fusion.3
  113.2 0.4 fusion.53
  113.5 1.5 collective-permute-start.8
  115.0 1.3 collective-permute-start.9
  116.3 0.7 copy.128
  117.3 31.3 %all-reduce.6.cloned.1.call-done = f32[96,1,7,7,7]{0,4,3,2,1:T(8,128)} async-done(((f32[96,1,7,7,7]{0,4,3,2,1:T(8,128)}), f32[96,1,7,7,7]{0,4,3,2,1:T(8,128)}) %all-reduce.6.cloned.1.call-update) | async-done | bytes 131728 | tf_op jit(solution)/shard_map/psum | solution.py:138
  148.7 0.7 pad_maximum_fusion.3
  149.4 2.1 collective-permute-start.10
  151.5 1.3 collective-permute-start.11
  152.9 7.5 %psum.58 = f32[96]{0:T(128)S(1)} all-reduce(f32[96]{0:T(128)S(1)} %broadcast_multiply_fusion.4), channel_id=1, replica_groups=mesh['groups'=2,'depth'=4,'rows'=2,'cols'=2] {'rows','cols'}, use_global_device_ids=true, to_apply=%region_7.0 | all-reduce | flops 96 | bytes 768 | tf_op jit(solution)/shard_map/psum | solution.py:138
  160.4 9.4 %psum.59 = f32[96]{0:T(128)} all-reduce(f32[96]{0:T(128)S(1)} %psum.58), channel_id=1, replica_groups=mesh['groups'=2,'depth'=4,'rows'=2,'cols'=2] {'depth'}, use_global_device_ids=true, to_apply=%region_8.0 | all-reduce | flops 96 | bytes 768 | tf_op jit(solution)/shard_map/psum | solution.py:138
  169.9 25.0 %all-reduce = (f32[192]{0:T(256)}, f32[384]{0:T(512)}) all-reduce(f32[192]{0:T(256)S(1)} %maximum_multiply_fusion, f32[384]{0:T(512)S(1)} %broadcast_multiply_fusion.3), channel_id=1, replica_groups=mesh['groups'=2,'depth'=4,'rows'=2,'cols'=2] {'depth','rows','cols'}, use_global_device_ids=true, to_apply=%region_11.0 | all-reduce | flops 576 | bytes 4608 | tf_op jit(solution)/shard_map/psum | solution.py:114
  194.9 1.8 copy.102
  196.7 7.8 %fusion.81 = bf16[2,10,14,22,96]{4,0,3,2,1:T(2,128)(2,1)S(1)} fusion(bf16[2,10,14,3,96]{4,0,3,2,1:T(2,128)(2,1)S(1)} %collective-permute-done.11, bf16[2,10,3,16,96]{4,0,3,2,1:T(2,128)(2,1)S(1)} %collective-permute-done.9, bf16[2,10,8,16,96]{4,0,3,2,1:T(2,128)(2,1)S(1)} %constant_dynamic-update-slice_fusion.3, ...), kind=kLoop, calls=%fused_computation.8.clone.1 | loop fusion | flops 2365440 | bytes 2365440 | tf_op jit(solution)/shard_map/conv_general_dilated | solution.py:28
  204.5 21.1 %fusion.4 = f32[2,4,8,16,96]{4,0,3,2,1:T(2,128)S(1)} fusion(bf16[96,1,7,7,7]{0,4,3,2,1:T(8,128)(2,1)S(1)} %copy-done.10, bf16[2,10,14,22,96]{4,0,3,2,1:T(2,128)(2,1)S(1)} %fusion.81), kind=kOutput, calls=%fused_computation.7 | convolution fusion | flops 67436544 | bytes 1641792 | tf_op jit(solution)/shard_map/conv_general_dilated | solution.py:28
  225.7 0.9 reshape.68
  226.6 56.0 %all-reduce.10.cloned.1.call-done = (f32[96,384]{1,0:T(8,128)}, f32[384,96]{0,1:T(8,128)}) async-done(((f32[96,384]{1,0:T(8,128)}, f32[384,96]{0,1:T(8,128)}), (f32[96,384]{1,0:T(8,128)}, f32[384,96]{0,1:T(8,128)})) %all-reduce.10.cloned.1.call-update) | async-done | bytes 294928 | tf_op jit(solution)/shard_map/psum | solution.py:114
  282.6 1.6 copy.137
  284.1 1.6 copy.138
  (71 shorter events, 3.7 us)
Async XLA Ops:
  7.2 18.8 %copy-start = (bf16[768,192]{0,1:T(8,128)(2,1)S(1)}, bf16[768,192]{0,1:T(8,128)(2,1)}, u32[]{:S(2)}) copy-start(bf16[768,192]{0,1:T(8,128)(2,1)} %param.15) | copy-start | bytes 884740
  7.2 7.6 %copy-start.3 = (bf16[2,4,8,1536]{3,2,1,0:T(8,128)(2,1)S(1)}, bf16[2,4,8,1536]{3,2,1,0:T(8,128)(2,1)}, u32[]{:S(2)}) copy-start(bf16[2,4,8,1536]{3,2,1,0:T(8,128)(2,1)} %param.11) | copy-start | bytes 589828
  7.2 8.1 %copy-start.6 = (bf16[768]{0:T(1024)(128)(2,1)S(1)}, bf16[768]{0:T(1024)(128)(2,1)}, u32[]{:S(2)}) copy-start(bf16[768]{0:T(1024)(128)(2,1)} %param.12) | copy-start | bytes 4612
  7.2 141.4 %all-reduce.6.cloned.1.call-start = ((), (), s32[]{:S(2)}) async-start(), calls=%async_computation | async-start | bytes 401408 | tf_op jit(solution)/shard_map/psum | solution.py:138
  8.7 8.5 %collective-permute-start = (bf16[2,3,8,16,96]{4,0,3,2,1:T(2,128)(2,1)S(1)}, bf16[2,3,8,16,96]{4,0,3,2,1:T(2,128)(2,1)S(1)}, u32[]{:S(2)}, u32[]{:S(2)}) collective-permute-start(bf16[2,3,8,16,96]{4,0,3,2,1:T(2,128)(2,1)S(1)} %copy.119), channel_id=1, source_target_pairs={{0,4},{4,8},{8,12},{1,5},{5,9},{9,13},{2,6},{6,10},{10,14},{3,7},{... | collective-permute-start | bytes 442376 | tf_op jit(solution)/shard_map/ppermute | solution.py:19
  12.5 8.3 %collective-permute-start.1 = (bf16[2,3,8,16,96]{4,0,3,2,1:T(2,128)(2,1)S(1)}, bf16[2,3,8,16,96]{4,0,3,2,1:T(2,128)(2,1)S(1)}, u32[]{:S(2)}, u32[]{:S(2)}) collective-permute-start(bf16[2,3,8,16,96]{4,0,3,2,1:T(2,128)(2,1)S(1)} %copy.120), channel_id=1, source_target_pairs={{4,0},{8,4},{12,8},{5,1},{9,5},{13,9},{6,2},{10,6},{14,10},{7,3},{... | collective-permute-start | bytes 442376 | tf_op jit(solution)/shard_map/ppermute | solution.py:22
  15.1 11.0 %copy-start.8 = (f32[192]{0:T(256)S(1)}, f32[192]{0:T(256)}, u32[]{:S(2)}) copy-start(f32[192]{0:T(256)} %param.16) | copy-start | bytes 2308
  21.2 7.5 %collective-permute-start.2 = (bf16[2,10,3,16,96]{4,0,3,2,1:T(2,128)(2,1)S(1)}, bf16[2,10,3,16,96]{4,0,3,2,1:T(2,128)(2,1)S(1)}, u32[]{:S(2)}, u32[]{:S(2)}) collective-permute-start(bf16[2,10,3,16,96]{4,0,3,2,1:T(2,128)(2,1)S(1)} %get-tuple-element.55), channel_id=1, source_target_pairs={{0,2},{1,3},{4,6},{5,7},{8,10},{9,11},{12,14},{13,15},{16,18},{17,... | collective-permute-start | bytes 552968 | tf_op jit(solution)/shard_map/ppermute | solution.py:19
  24.6 8.2 %collective-permute-start.3 = (bf16[2,10,3,16,96]{4,0,3,2,1:T(2,128)(2,1)S(1)}, bf16[2,10,3,16,96]{4,0,3,2,1:T(2,128)(2,1)S(1)}, u32[]{:S(2)}, u32[]{:S(2)}) collective-permute-start(bf16[2,10,3,16,96]{4,0,3,2,1:T(2,128)(2,1)S(1)} %get-tuple-element.56), channel_id=1, source_target_pairs={{2,0},{3,1},{6,4},{7,5},{10,8},{11,9},{14,12},{15,13},{18,16},{19,... | collective-permute-start | bytes 552968 | tf_op jit(solution)/shard_map/ppermute | solution.py:22
  33.5 2.9 %collective-permute-start.4 = (bf16[2,10,14,3,96]{4,0,3,2,1:T(2,128)(2,1)S(1)}, bf16[2,10,14,3,96]{4,0,3,2,1:T(2,128)(2,1)S(1)}, u32[]{:S(2)}, u32[]{:S(2)}) collective-permute-start(bf16[2,10,14,3,96]{4,0,3,2,1:T(2,128)(2,1)S(1)} %get-tuple-element.51), channel_id=1, source_target_pairs={{0,1},{2,3},{4,5},{6,7},{8,9},{10,11},{12,13},{14,15},{16,17},{18,... | collective-permute-start | bytes 483848 | tf_op jit(solution)/shard_map/ppermute | solution.py:19
  34.8 3.4 %collective-permute-start.5 = (bf16[2,10,14,3,96]{4,0,3,2,1:T(2,128)(2,1)S(1)}, bf16[2,10,14,3,96]{4,0,3,2,1:T(2,128)(2,1)S(1)}, u32[]{:S(2)}, u32[]{:S(2)}) collective-permute-start(bf16[2,10,14,3,96]{4,0,3,2,1:T(2,128)(2,1)S(1)} %get-tuple-element.52), channel_id=1, source_target_pairs={{1,0},{3,2},{5,4},{7,6},{9,8},{11,10},{13,12},{15,14},{17,16},{19,... | collective-permute-start | bytes 483848 | tf_op jit(solution)/shard_map/ppermute | solution.py:22
  36.5 9.5 %copy-start.9 = (bf16[96,1,7,7,7]{0,4,3,2,1:T(8,128)(2,1)S(1)}, bf16[96,1,7,7,7]{0,4,3,2,1:T(8,128)(2,1)}, u32[]{:S(2)}) copy-start(bf16[96,1,7,7,7]{0,4,3,2,1:T(8,128)(2,1)} %param.13) | copy-start | bytes 197572
  36.5 9.5 %copy-start.12 = (f32[96]{0:T(128)S(1)}, f32[96]{0:T(128)}, u32[]{:S(2)}) copy-start(f32[96]{0:T(128)} %param.14) | copy-start | bytes 1156
  46.0 19.1 %copy-start.1 = (bf16[2,10,14,22,96]{4,0,3,2,1:T(2,128)(2,1)}, bf16[2,10,14,22,96]{4,0,3,2,1:T(2,128)(2,1)S(1)}, u32[]{:S(2)}) copy-start(bf16[2,10,14,22,96]{4,0,3,2,1:T(2,128)(2,1)S(1)} %pad_maximum_fusion) | copy-start | bytes 3548164
  65.1 0.9 copy-start.4
  65.1 0.9 copy-start.7
  66.5 1.4 copy-start.11
  87.1 7.1 %copy-start.2 = (bf16[2,10,14,22,96]{4,0,3,2,1:T(2,128)(2,1)S(1)}, bf16[2,10,14,22,96]{4,0,3,2,1:T(2,128)(2,1)}, u32[]{:S(2)}) copy-start(bf16[2,10,14,22,96]{4,0,3,2,1:T(2,128)(2,1)} %copy-done.1) | copy-start | bytes 3548164
  87.3 23.3 %collective-permute-start.6 = (bf16[2,3,8,16,96]{4,0,3,2,1:T(2,128)(2,1)S(1)}, bf16[2,3,8,16,96]{4,0,3,2,1:T(2,128)(2,1)}, u32[]{:S(2)}, u32[]{:S(2)}) collective-permute-start(bf16[2,3,8,16,96]{4,0,3,2,1:T(2,128)(2,1)S(1)} %copy.121), channel_id=1, source_target_pairs={{0,4},{4,8},{8,12},{1,5},{5,9},{9,13},{2,6},{6,10},{10,14},{3,7},{... | collective-permute-start | bytes 442376 | tf_op jit(solution)/shard_map/ppermute | solution.py:19
  91.2 20.9 %collective-permute-start.7 = (bf16[2,3,8,16,96]{4,0,3,2,1:T(2,128)(2,1)S(1)}, bf16[2,3,8,16,96]{4,0,3,2,1:T(2,128)(2,1)}, u32[]{:S(2)}, u32[]{:S(2)}) collective-permute-start(bf16[2,3,8,16,96]{4,0,3,2,1:T(2,128)(2,1)S(1)} %copy.122), channel_id=1, source_target_pairs={{4,0},{8,4},{12,8},{5,1},{9,5},{13,9},{6,2},{10,6},{14,10},{7,3},{... | collective-permute-start | bytes 442376 | tf_op jit(solution)/shard_map/ppermute | solution.py:22
  110.7 5.6 %copy-start.5 = (f32[1,7,7,7,96]{4,0,3,2,1:T(1,128)S(1)}, f32[1,7,7,7,96]{4,0,3,2,1:T(1,128)}, u32[]{:S(2)}) copy-start(f32[1,7,7,7,96]{4,0,3,2,1:T(1,128)} %fusion.26) | copy-start | bytes 395140
  113.5 35.1 %collective-permute-start.8 = (bf16[2,10,3,16,96]{4,0,3,2,1:T(2,128)(2,1)S(1)}, bf16[2,10,3,16,96]{4,0,3,2,1:T(2,128)(2,1)S(1)}, u32[]{:S(2)}, u32[]{:S(2)}) collective-permute-start(bf16[2,10,3,16,96]{4,0,3,2,1:T(2,128)(2,1)S(1)} %get-tuple-element.53), channel_id=1, source_target_pairs={{0,2},{1,3},{4,6},{5,7},{8,10},{9,11},{12,14},{13,15},{16,18},{17,... | collective-permute-start | bytes 552968 | tf_op jit(solution)/shard_map/ppermute | solution.py:19
  115.0 33.7 %collective-permute-start.9 = (bf16[2,10,3,16,96]{4,0,3,2,1:T(2,128)(2,1)S(1)}, bf16[2,10,3,16,96]{4,0,3,2,1:T(2,128)(2,1)S(1)}, u32[]{:S(2)}, u32[]{:S(2)}) collective-permute-start(bf16[2,10,3,16,96]{4,0,3,2,1:T(2,128)(2,1)S(1)} %get-tuple-element.54), channel_id=1, source_target_pairs={{2,0},{3,1},{6,4},{7,5},{10,8},{11,9},{14,12},{15,13},{18,16},{19,... | collective-permute-start | bytes 552968 | tf_op jit(solution)/shard_map/ppermute | solution.py:22
  117.0 77.9 %all-reduce.8.cloned.1.call-start = ((), (), s32[]{:S(2)}) async-start(), calls=%async_computation.1 | async-start | bytes 401408 | tf_op jit(solution)/shard_map/psum | solution.py:138
  148.6 134.0 %all-reduce.10.cloned.1.call-start = ((), (), s32[]{:S(2)}) async-start(), calls=%async_computation.2 | async-start | bytes 589824 | tf_op jit(solution)/shard_map/psum | solution.py:114
  149.4 47.3 %collective-permute-start.10 = (bf16[2,10,14,3,96]{4,0,3,2,1:T(2,128)(2,1)S(1)}, bf16[2,10,14,3,96]{4,0,3,2,1:T(2,128)(2,1)S(1)}, u32[]{:S(2)}, u32[]{:S(2)}) collective-permute-start(bf16[2,10,14,3,96]{4,0,3,2,1:T(2,128)(2,1)S(1)} %get-tuple-element.49), channel_id=1, source_target_pairs={{0,1},{2,3},{4,5},{6,7},{8,9},{10,11},{12,13},{14,15},{16,17},{18,... | collective-permute-start | bytes 483848 | tf_op jit(solution)/shard_map/ppermute | solution.py:19
  151.5 45.2 %collective-permute-start.11 = (bf16[2,10,14,3,96]{4,0,3,2,1:T(2,128)(2,1)S(1)}, bf16[2,10,14,3,96]{4,0,3,2,1:T(2,128)(2,1)S(1)}, u32[]{:S(2)}, u32[]{:S(2)}) collective-permute-start(bf16[2,10,14,3,96]{4,0,3,2,1:T(2,128)(2,1)S(1)} %get-tuple-element.50), channel_id=1, source_target_pairs={{1,0},{3,2},{5,4},{7,6},{9,8},{11,10},{13,12},{15,14},{17,16},{19,... | collective-permute-start | bytes 483848 | tf_op jit(solution)/shard_map/ppermute | solution.py:22
  196.7 7.8 %copy-start.10 = (bf16[96,1,7,7,7]{0,4,3,2,1:T(8,128)(2,1)S(1)}, bf16[96,1,7,7,7]{0,4,3,2,1:T(8,128)(2,1)}, u32[]{:S(2)}) copy-start(bf16[96,1,7,7,7]{0,4,3,2,1:T(8,128)(2,1)} %param.13) | copy-start | bytes 197572
Sparse Core Ops, SparseCore 0:
  117.1 31.3 all-reduce.5
  150.9 36.6 all-reduce.7
  191.6 90.8 all-reduce.9
